TPU v7x, 32 devices: a whole 2x2x4 slice. The times are simulated.
32 devices in a mesh: pts: 4 (over x, core), snap: 8 (over z, y).
Axes of the slice: x: 2, y: 2, z: 4, core: 2. Of those that a mesh axis runs over, the one named last changes fastest.
Arguments:
- snapshots: float32 [4096, 8192], P('pts', 'snap'), may hold values from -8 to 8
- modes_init: float32 [4096, 128], P('pts'), may hold values from -6 to 6
- coefs_init: float32 [128, 8192], P(None, 'snap'), may hold values from -0.09375 to 0.09375
Outputs:
- modes: float32 [4096, 128], P('pts')
- amplitudes: float32 [128, 8192], P(None, 'snap')
All inputs are finite; a program needn't handle non-finite values.
Results may differ from a plain program's by a relative error of at most 0.0003.
Values sent between devices are 32-bit elements; how exact they have to be, the bound alone decides.
A program may use at most 64 MiB of HBM per device.

v0:
```python
import jax
import jax.numpy as jnp
from jax import lax
from jax.sharding import PartitionSpec as P

OUTER = 2
INNER = 2


HUBER = 1.345
RIDGE = 0.01


def high_dot(left, right):
    return jnp.dot(left, right, preferred_element_type=jnp.float32, precision=lax.Precision.HIGHEST)


def clipped_error(snapshots, modes, coefs, count):
    error = snapshots - high_dot(modes, coefs)
    total = lax.psum(jnp.sum(error * error), ("pts", "snap"))
    limit = HUBER * jnp.sqrt(total / count + 1e-06)
    return jnp.clip(error, -limit, limit)


def shards(snapshots, modes_init, coefs_init):
    modes = modes_init
    coefs = coefs_init
    rows, width = snapshots.shape
    points = rows * lax.axis_size("pts")
    count = float(points * width * lax.axis_size("snap"))
    rank = modes.shape[1]
    eye = jnp.eye(rank, dtype=jnp.float32)
    for outer in range(OUTER):
        gram = lax.psum(high_dot(modes.T, modes), "pts") + RIDGE * eye
        factor = jnp.linalg.cholesky(gram)
        for inner in range(INNER):
            clipped = clipped_error(snapshots, modes, coefs, count)
            product = high_dot(modes.T, clipped)
            share = lax.psum_scatter(product, "pts", scatter_dimension=1, tiled=True)
            span = share.shape[1]
            own = lax.dynamic_slice_in_dim(coefs, lax.axis_index("pts") * span, span, 1)
            own = own + jax.scipy.linalg.cho_solve((factor, True), share)
            coefs = lax.all_gather(own, "pts", axis=1, tiled=True)
        clipped = clipped_error(snapshots, modes, coefs, count)
        hess = lax.psum(high_dot(coefs, coefs.T), "snap") + RIDGE * eye
        hfactor = jnp.linalg.cholesky(hess)
        moment = high_dot(clipped, coefs.T)
        summed = lax.psum(moment, "snap")
        modes = modes + jax.scipy.linalg.cho_solve((hfactor, True), summed.T).T
    return (modes, coefs * jnp.sqrt(jnp.float32(points)))


def solution(mesh):
    in_specs = (P("pts", "snap"), P("pts", None), P(None, "snap"))
    out_specs = (P("pts", None), P(None, "snap"))
    return jax.shard_map(shards, mesh=mesh, in_specs=in_specs, out_specs=out_specs, check_vma=False)
```

profile of v0, /device:TPU:0, one launch (start us, length us, event | category | flops | bytes accessed | tf_op | source)
XLA Modules:
  0.0 691.9 jit_solution(7492501816023668363)
XLA Ops:
  10.1 8.6 %multiply_reduce_fusion.5 = (f32[]{:T(128)}, f32[1024,1024]{1,0:T(8,128)}) fusion(f32[1024,1024]{1,0:T(8,128)} %param.8, f32[1024,128]{1,0:T(8,128)} %param.9, f32[128,1024]{1,0:T(8,128)} %param.10), kind=kOutput, calls=%fused_computation.25 | convolution fusion | flops 1613758464 | bytes 9437188 | tf_op jit(solution)/shard_map/dot_general | solution.py:15
  18.8 42.7 %psum.85 = f32[]{:T(128)} all-reduce(f32[]{:T(128)} %get-tuple-element.11), channel_id=1, replica_groups=mesh['pts'=4,'snap'=8] {'pts','snap'}, use_global_device_ids=true, to_apply=%region_4.6 | all-reduce | flops 1 | bytes 8 | tf_op jit(solution)/shard_map/psum | solution.py:20
  62.2 9.6 %fusion.32 = f32[128,1024]{0,1:T(8,128)} fusion(f32[1024,128]{1,0:T(8,128)S(1)} %copy-done, f32[1024,1024]{1,0:T(8,128)} %get-tuple-element.12, f32[]{:T(128)S(6)} %neg.18, f32[]{:T(128)S(6)} %mul.63), kind=kOutput, calls=%fused_computation.46 | convolution fusion | flops 1612709888 | bytes 5242888 | tf_op jit(solution)/shard_map/dot_general | solution.py:15
  79.2 11.7 %cholesky.74 = f32[128,128]{1,0:T(8,128)S(1)} custom-call(f32[128,128]{1,0:T(8,128)S(1)} %fusion.63), custom_call_target="Cholesky" | custom-call | tf_op jit(solution)/shard_map/jit(cholesky)/cholesky | solution.py:35
  92.3 9.8 %custom-call.16 = f32[1,128,128]{1,2,0:T(8,128)S(1)} custom-call(f32[1,128,128]{2,1,0:T(8,128)S(1)} %fusion.38), custom_call_target="InvertDiagBlocksLowerTriangular" | custom-call | tf_op jit(solution)/shard_map/jit(_cho_solve)/triangular_solve | solution.py:42
  104.5 8.0 %all_gather.12 = f32[128,1024]{1,0:T(8,128)S(1)} all-gather(f32[128,256]{1,0:T(8,128)S(1)} %convolution_add_fusion.3), channel_id=1, replica_groups=mesh['pts'=4,'snap'=8] {'pts'}, dimensions={1}, use_global_device_ids=true | all-gather | bytes 655360 | tf_op jit(solution)/shard_map/all_gather | solution.py:43
  112.5 7.7 %multiply_reduce_fusion.4 = (f32[]{:T(128)}, f32[1024,1024]{0,1:T(8,128)}) fusion(f32[1024,1024]{0,1:T(8,128)} %copy.7, f32[128,1024]{1,0:T(8,128)S(1)} %all_gather.12, f32[1024,128]{1,0:T(8,128)S(1)} %copy-done), kind=kOutput, calls=%fused_computation.21 | convolution fusion | flops 1613758464 | bytes 9437188 | tf_op jit(solution)/shard_map/dot_general | solution.py:15
  120.2 39.8 %psum.86 = f32[]{:T(128)} all-reduce(f32[]{:T(128)} %get-tuple-element.13), channel_id=1, replica_groups=mesh['pts'=4,'snap'=8] {'pts','snap'}, use_global_device_ids=true, to_apply=%region_7.10 | all-reduce | flops 1 | bytes 8 | tf_op jit(solution)/shard_map/psum | solution.py:20
  160.7 6.4 fusion.35
  167.1 22.0 %reduce-scatter.7.cloned.1.call-done = f32[128,256]{0,1:T(8,128)} async-done(((f32[128,1024]{0,1:T(8,128)}), f32[128,256]{0,1:T(8,128)}) %reduce-scatter.7.cloned.1.call-update) | async-done | bytes 131088 | tf_op jit(solution)/shard_map/reduce_scatter | solution.py:39
  190.6 6.6 all_gather.13
  197.2 7.6 %multiply_reduce_fusion.3 = (f32[]{:T(128)}, f32[1024,1024]{0,1:T(8,128)}) fusion(f32[1024,1024]{0,1:T(8,128)} %copy.7, f32[128,1024]{1,0:T(8,128)S(1)} %all_gather.13, f32[1024,128]{1,0:T(8,128)S(1)} %copy-done), kind=kOutput, calls=%fused_computation.17 | convolution fusion | flops 1613758464 | bytes 9437188 | tf_op jit(solution)/shard_map/dot_general | solution.py:15
  206.0 40.0 %psum.88 = f32[]{:T(128)} all-reduce(f32[]{:T(128)} %get-tuple-element.15), channel_id=1, replica_groups=mesh['pts'=4,'snap'=8] {'pts','snap'}, use_global_device_ids=true, to_apply=%region_11.14 | all-reduce | flops 1 | bytes 8 | tf_op jit(solution)/shard_map/psum | solution.py:20
  253.1 73.1 %all-reduce.13.cloned.1.call-done = (f32[128,1024]{1,0:T(8,128)}, f32[128,128]{0,1:T(8,128)}) async-done(((f32[128,1024]{1,0:T(8,128)}, f32[128,128]{0,1:T(8,128)}), (f32[128,1024]{1,0:T(8,128)}, f32[128,128]{0,1:T(8,128)})) %all-reduce.13.cloned.1.call-update) | async-done | bytes 589840 | tf_op jit(solution)/shard_map/psum | solution.py:48
  328.1 11.7 %cholesky.85 = f32[128,128]{1,0:T(8,128)S(1)} custom-call(f32[128,128]{1,0:T(8,128)S(1)} %fusion.56), custom_call_target="Cholesky" | custom-call | tf_op jit(solution)/shard_map/jit(cholesky)/cholesky | solution.py:46
  341.1 9.8 %custom-call.18 = f32[1,128,128]{1,2,0:T(8,128)S(1)} custom-call(f32[1,128,128]{2,1,0:T(8,128)S(1)} %fusion.39), custom_call_target="InvertDiagBlocksLowerTriangular" | custom-call | tf_op jit(solution)/shard_map/jit(_cho_solve)/triangular_solve | solution.py:49
  354.4 7.6 %multiply_reduce_fusion.2 = (f32[]{:T(128)}, f32[1024,1024]{1,0:T(8,128)}) fusion(f32[1024,1024]{1,0:T(8,128)} %param.8, f32[1024,128]{0,1:T(8,128)S(1)} %fusion.30, f32[128,1024]{1,0:T(8,128)S(1)} %all_gather.13), kind=kOutput, calls=%fused_computation.13 | convolution fusion | flops 1613758464 | bytes 9437188 | tf_op jit(solution)/shard_map/dot_general | solution.py:15
  362.1 39.8 %psum.91 = f32[]{:T(128)} all-reduce(f32[]{:T(128)} %get-tuple-element.17), channel_id=1, replica_groups=mesh['pts'=4,'snap'=8] {'pts','snap'}, use_global_device_ids=true, to_apply=%region_15.19 | all-reduce | flops 1 | bytes 8 | tf_op jit(solution)/shard_map/psum | solution.py:20
  410.1 11.7 %cholesky.96 = f32[128,128]{1,0:T(8,128)S(1)} custom-call(f32[128,128]{1,0:T(8,128)S(1)} %fusion.52), custom_call_target="Cholesky" | custom-call | tf_op jit(solution)/shard_map/jit(cholesky)/cholesky | solution.py:35
  423.2 9.8 %custom-call.19 = f32[1,128,128]{1,2,0:T(8,128)S(1)} custom-call(f32[1,128,128]{2,1,0:T(8,128)S(1)} %fusion.40), custom_call_target="InvertDiagBlocksLowerTriangular" | custom-call | tf_op jit(solution)/shard_map/jit(_cho_solve)/triangular_solve | solution.py:42
  434.5 8.2 %all_gather.14 = f32[128,1024]{1,0:T(8,128)S(1)} all-gather(f32[128,256]{1,0:T(8,128)S(1)} %convolution_add_fusion.1), channel_id=1, replica_groups=mesh['pts'=4,'snap'=8] {'pts'}, dimensions={1}, use_global_device_ids=true | all-gather | bytes 655360 | tf_op jit(solution)/shard_map/all_gather | solution.py:43
  442.7 7.6 %multiply_reduce_fusion.1 = (f32[]{:T(128)}, f32[1024,1024]{1,0:T(8,128)}) fusion(f32[1024,1024]{1,0:T(8,128)} %param.8, f32[1024,128]{0,1:T(8,128)S(1)} %fusion.30, f32[128,1024]{1,0:T(8,128)S(1)} %all_gather.14), kind=kOutput, calls=%fused_computation.9 | convolution fusion | flops 1613758464 | bytes 9437188 | tf_op jit(solution)/shard_map/dot_general | solution.py:15
  450.3 38.7 %psum.92 = f32[]{:T(128)} all-reduce(f32[]{:T(128)} %get-tuple-element.19), channel_id=1, replica_groups=mesh['pts'=4,'snap'=8] {'pts','snap'}, use_global_device_ids=true, to_apply=%region_18.22 | all-reduce | flops 1 | bytes 8 | tf_op jit(solution)/shard_map/psum | solution.py:20
  489.7 5.7 fusion.3
  495.4 22.4 %reduce-scatter.11.cloned.1.call-done = f32[128,256]{1,0:T(8,128)} async-done(((f32[128,1024]{1,0:T(8,128)}), f32[128,256]{1,0:T(8,128)}) %reduce-scatter.11.cloned.1.call-update) | async-done | bytes 131088 | tf_op jit(solution)/shard_map/reduce_scatter | solution.py:39
  519.3 6.6 all_gather.15
  525.9 7.6 %multiply_reduce_fusion = (f32[]{:T(128)}, f32[1024,1024]{1,0:T(8,128)}) fusion(f32[1024,1024]{1,0:T(8,128)} %param.8, f32[1024,128]{0,1:T(8,128)S(1)} %fusion.30, f32[128,1024]{1,0:T(8,128)S(1)} %all_gather.15), kind=kOutput, calls=%fused_computation.5 | convolution fusion | flops 1613758464 | bytes 9437188 | tf_op jit(solution)/shard_map/dot_general | solution.py:15
  534.7 40.3 %psum.94 = f32[]{:T(128)} all-reduce(f32[]{:T(128)} %get-tuple-element.21), channel_id=1, replica_groups=mesh['pts'=4,'snap'=8] {'pts','snap'}, use_global_device_ids=true, to_apply=%region_22.26 | all-reduce | flops 1 | bytes 8 | tf_op jit(solution)/shard_map/psum | solution.py:20
  575.7 7.3 %fusion = f32[128,1024]{1,0:T(8,128)} fusion(f32[128,1024]{1,0:T(8,128)S(1)} %all_gather.15, f32[1024,1024]{1,0:T(8,128)} %get-tuple-element.22, f32[]{:T(128)S(6)} %neg.23, f32[]{:T(128)S(6)} %mul.73), kind=kOutput, calls=%fused_computation.2 | convolution fusion | flops 1612709888 | bytes 5242888 | tf_op jit(solution)/shard_map/dot_general | solution.py:15
  583.9 73.0 %all-reduce.11.cloned.1.call-done = (f32[128,1024]{1,0:T(8,128)}, f32[128,128]{0,1:T(8,128)}) async-done(((f32[128,1024]{1,0:T(8,128)}, f32[128,128]{0,1:T(8,128)}), (f32[128,1024]{1,0:T(8,128)}, f32[128,128]{0,1:T(8,128)})) %all-reduce.11.cloned.1.call-update) | async-done | bytes 589840 | tf_op jit(solution)/shard_map/psum | solution.py:48
  658.6 11.7 %cholesky.107 = f32[128,128]{1,0:T(8,128)S(1)} custom-call(f32[128,128]{1,0:T(8,128)S(1)} %fusion.45), custom_call_target="Cholesky" | custom-call | tf_op jit(solution)/shard_map/jit(cholesky)/cholesky | solution.py:46
  671.7 9.8 %custom-call.21 = f32[1,128,128]{1,2,0:T(8,128)S(1)} custom-call(f32[1,128,128]{2,1,0:T(8,128)S(1)} %fusion.41), custom_call_target="InvertDiagBlocksLowerTriangular" | custom-call | tf_op jit(solution)/shard_map/jit(_cho_solve)/triangular_solve | solution.py:49
  (68 shorter events, 50.2 us)
Async XLA Ops:
  7.2 70.3 %all-reduce.7.cloned.1.call-start = ((), (), s32[]{:S(2)}) async-start(), calls=%async_computation.4 | async-start | bytes 131072 | tf_op jit(solution)/shard_map/psum | solution.py:34
  10.1 52.1 %copy-start = (f32[1024,128]{1,0:T(8,128)S(1)}, f32[1024,128]{1,0:T(8,128)}, u32[]{:S(2)}) copy-start(f32[1024,128]{1,0:T(8,128)} %param.9) | copy-start | bytes 1572868
  10.1 92.1 %reduce-scatter.5.cloned.1.call-start = ((), (), s32[]{:S(2)}) async-start(), calls=%async_computation.5 | async-start | bytes 655360 | tf_op jit(solution)/shard_map/reduce_scatter | solution.py:39
  71.8 117.3 %reduce-scatter.7.cloned.1.call-start = ((), (), s32[]{:S(2)}) async-start(), calls=%async_computation.6 | async-start | bytes 655360 | tf_op jit(solution)/shard_map/reduce_scatter | solution.py:39
  167.1 159.2 %all-reduce.13.cloned.1.call-start = ((), (), s32[]{:S(2)}) async-start(), calls=%async_computation.11 | async-start | bytes 1179648 | tf_op jit(solution)/shard_map/psum | solution.py:48
  252.5 155.8 %all-reduce.9.cloned.1.call-start = ((), (), s32[]{:S(2)}) async-start(), calls=%async_computation.7 | async-start | bytes 131072 | tf_op jit(solution)/shard_map/psum | solution.py:34
  362.0 71.0 %reduce-scatter.9.cloned.1.call-start = ((), (), s32[]{:S(2)}) async-start(), calls=%async_computation.8 | async-start | bytes 655360 | tf_op jit(solution)/shard_map/reduce_scatter | solution.py:39
  408.2 109.6 %reduce-scatter.11.cloned.1.call-start = ((), (), s32[]{:S(2)}) async-start(), calls=%async_computation.9 | async-start | bytes 655360 | tf_op jit(solution)/shard_map/reduce_scatter | solution.py:39
  495.4 161.4 %all-reduce.11.cloned.1.call-start = ((), (), s32[]{:S(2)}) async-start(), calls=%async_computation.10 | async-start | bytes 1179648 | tf_op jit(solution)/shard_map/psum | solution.py:48
Sparse Core Ops, SparseCore 0:
  10.9 34.2 all-reduce.6
  71.9 21.7 reduce-scatter.4
  167.2 21.8 reduce-scatter.6
  252.6 73.6 all-reduce.12
  362.1 30.6 all-reduce.8
  408.4 21.7 reduce-scatter.8
  495.5 22.2 reduce-scatter.10
  583.1 73.6 all-reduce.10
where the time goes:
time: 698 us; the launch traced here: 692 us
  blocking collectives  271 us (39%)
  waiting for transfers between devices  191 us (27%)
  matrix products  105 us (15%)
  other arithmetic  99.1 us (14%)
  between operations  18.9 us (3%)
    psum x6, blocking collectives, clipped_error(): total = lax.psum(jnp.sum(error * error), ('pts', 'snap'))  241 us
    psum x2, waiting for transfers between devices, shards(): summed = lax.psum(moment, 'snap')  146 us
    dot_general x16, matrix products, high_dot(): jnp.dot(left, right, preferred_element_type=jnp.float32, precision=lax.Pr...  93.5 us
    reduce_scatter x4, waiting for transfers between devices, shards(): share = lax.psum_scatter(product, 'pts', scatter_dimension=1, tiled=True)  44.4 us
    all_gather x4, blocking collectives, shards(): coefs = lax.all_gather(own, 'pts', axis=1, tiled=True)  29.3 us
    another operation x6, other arithmetic, shards(): factor = jnp.linalg.cholesky(gram)  24.8 us
    another operation x6, other arithmetic, shards(): hfactor = jnp.linalg.cholesky(hess)  24.8 us
    another operation x4, other arithmetic, shards(): own = own + jax.scipy.linalg.cho_solve((factor, True), share)  20.9 us
  transfers between devices with their start and end apart: 8, of which 4 were waited for; matrix products, arithmetic and copies ran while one was open for 12% of the time, Pallas kernels for 0%

commit v1 on v0

v1 whole, which is shorter than its diff:
```python
import functools

import jax
import jax.numpy as jnp
from jax import lax
from jax.experimental import pallas as pl
from jax.experimental.pallas import tpu as pltpu
from jax.sharding import PartitionSpec as P

OUTER = 2
INNER = 2

HUBER = 1.345
RIDGE = 0.01

F32 = jnp.float32
BF16 = jnp.bfloat16
MESH = pl.DeviceIdType.MESH


def split(x):
    hi = x.astype(BF16)
    lo = (x - hi.astype(F32)).astype(BF16)
    return hi, lo


def dot(a, b):
    return jnp.dot(a, b, preferred_element_type=F32)


def quads(x):
    r, c = x.shape[0] // 2, x.shape[1] // 2
    return (x[:r, :c] + x[:r, c:]) + (x[r:, :c] + x[r:, c:])


def pts_peer(me, j, n):
    if n % 2:
        return lax.rem(me + j, n)
    x, c = me // 2, lax.rem(me, 2)
    return lax.rem(x + j // 2, n // 2) * 2 + lax.rem(c + lax.rem(j, 2), 2)


def snap_peer(me, j, n):
    return lax.rem(me + j, n)


def kernel(n_pts, n_snap, s_hbm, m_in, c_in, m_out, c_out,
           s, e, mcat, mtcat, ccat, ctcat, sq,
           gpart, gslots, gred, gfull, hpart, hslots, hred, hfull,
           tile_p, slots_p, tile_s, slots_s, proj, proj_slots, mom, mom_slots,
           load_sem, p_send, p_recv, s_send, s_recv):
    rows, width = s.shape
    rank = m_in.shape[1]
    pme = lax.axis_index("pts")
    sme = lax.axis_index("snap")
    cw = width // n_pts
    rw = rows // n_snap
    gw = rank // n_pts
    hw = rank // n_snap
    points = float(rows * n_pts)
    count = float(rows * n_pts * width * n_snap)
    step_cols = 256
    own_cols = pl.ds(pl.multiple_of(pme * cw, cw), cw)
    own_rows = pl.ds(pl.multiple_of(sme * rw, rw), rw)

    load = pltpu.make_async_copy(s_hbm, s, load_sem)
    load.start()

    barrier = pltpu.get_barrier_semaphore()
    for j in range(1, n_pts):
        pl.semaphore_signal(barrier, inc=1, device_id={"pts": pts_peer(pme, j, n_pts)}, device_id_type=MESH)
    for j in range(1, n_snap):
        pl.semaphore_signal(barrier, inc=1, device_id={"snap": snap_peer(sme, j, n_snap)}, device_id_type=MESH)
    m_out[...] = m_in[...]
    c_out[...] = c_in[...]
    pl.semaphore_wait(barrier, n_pts - 1 + n_snap - 1)

    def pcopy(site, j, src, dst):
        return pltpu.make_async_remote_copy(
            src_ref=src, dst_ref=dst, send_sem=p_send.at[site, j - 1], recv_sem=p_recv.at[site, j - 1],
            device_id={"pts": pts_peer(pme, j, n_pts)}, device_id_type=MESH)

    def scopy(site, j, src, dst):
        return pltpu.make_async_remote_copy(
            src_ref=src, dst_ref=dst, send_sem=s_send.at[site, j - 1], recv_sem=s_recv.at[site, j - 1],
            device_id={"snap": snap_peer(sme, j, n_snap)}, device_id_type=MESH)

    def start(copies):
        for copy in copies:
            copy.start()

    def finish(copies):
        for copy in copies:
            copy.wait_recv()
        for copy in copies:
            copy.wait_send()

    def prepare_modes():
        m = m_out[...]
        hi, lo = split(m)
        mcat[:, :rank] = hi
        mcat[:, rank:] = lo
        hi, lo = split(m.T)
        mtcat[:rank, :] = hi
        mtcat[rank:, :] = lo

    def prepare_coefs():
        hi, lo = split(c_out[...])
        ccat[:rank, :] = hi
        ccat[rank:, :] = lo

    def sweep(ref, lo, hi):
        lane = lax.broadcasted_iota(jnp.int32, (rank, rank), 1)
        sub = lax.broadcasted_iota(jnp.int32, (rank, rank), 0)
        lane_row = lax.broadcasted_iota(jnp.int32, (1, rank), 1)

        def body(k, carry):
            full = ref[...]
            row = ref[pl.ds(k, 1), :]
            pivot = jnp.sum(jnp.where(lane_row == k, row, 0.0), axis=1, keepdims=True)
            col = jnp.sum(jnp.where(lane == k, full, 0.0), axis=1, keepdims=True)
            inv = 1.0 / pivot
            rowd = jnp.where(lane_row == k, -inv, row * inv)
            new = full - col * (row * inv)
            new = jnp.where(lane == k, col * inv, new)
            ref[...] = jnp.where(sub == k, rowd, new)
            return carry
        lax.fori_loop(lo, hi, body, 0)

    def error_pass():
        sq[...] = jnp.zeros_like(sq)

        def body(t, carry):
            cols = pl.ds(pl.multiple_of(t * step_cols, step_cols), step_cols)
            c = ccat[:, cols]
            hi, lo = mcat[:, :rank], mcat[:, rank:]
            fit = dot(jnp.concatenate([hi, hi], 1), c) + dot(jnp.concatenate([lo, lo], 1), c)
            err = s[:, cols] - fit
            e[:, cols] = err
            sq[...] += jnp.sum((err * err).reshape(rows // 8, 8, step_cols), axis=0)
            return carry
        lax.fori_loop(0, width // step_cols, body, 0)
        acc = sq[:, :128]
        for k in range(1, step_cols // 128):
            acc = acc + sq[:, k * 128:(k + 1) * 128]
        return acc

    def find_limit(use, acc, fill_p, fill_s):
        tile_p[use] = acc
        copies = [pcopy(use, j, tile_p.at[use], slots_p.at[use, j - 1]) for j in range(1, n_pts)]
        start(copies)
        fill_p()
        finish(copies)
        acc = tile_p[use]
        for j in range(1, n_pts):
            acc = acc + slots_p[use, j - 1]
        tile_s[use] = acc
        copies = [scopy(use, j, tile_s.at[use], slots_s.at[use, j - 1]) for j in range(1, n_snap)]
        start(copies)
        fill_s()
        finish(copies)
        acc = tile_s[use]
        for j in range(1, n_snap):
            acc = acc + slots_s[use, j - 1]
        total = jnp.sum(jnp.sum(acc, axis=0, keepdims=True), axis=1, keepdims=True)
        return HUBER * jnp.sqrt(total / count + 1e-06)

    def nothing():
        return None

    eye = (lax.broadcasted_iota(jnp.int32, (rank, rank), 0)
           == lax.broadcasted_iota(jnp.int32, (rank, rank), 1)).astype(F32) * RIDGE

    prepare_modes()
    prepare_coefs()
    load.wait()

    def outer(o, carry):
        gpart[...] = quads(dot(mtcat[...], mcat[...]))
        grs = [pcopy(3, j, gpart.at[pl.ds(pts_peer(pme, j, n_pts) * gw, gw)], gslots.at[j - 1]) for j in range(1, n_pts)]
        start(grs)
        gag = [pcopy(4, j, gred, gfull.at[pl.ds(pme * gw, gw)]) for j in range(1, n_pts)]

        for inner in range(INNER):
            acc = error_pass()

            def gram_share():
                finish(grs)
                own = gpart[pl.ds(pme * gw, gw), :]
                for j in range(1, n_pts):
                    own = own + gslots[j - 1]
                gred[...] = own
                gfull[pl.ds(pme * gw, gw), :] = own
                start(gag)

            def gram_sweep():
                finish(gag)
                gfull[...] = gfull[...] + eye
                sweep(gfull, 0, rank // 2)
            first = inner == 0
            limit = find_limit(inner, acc, gram_share if first else nothing, gram_sweep if first else nothing)

            def project(t, carry):
                j = n_pts - 1 - t
                q = pts_peer(pme, j, n_pts)
                cols = pl.ds(pl.multiple_of(q * cw, cw), cw)
                hi, lo = split(jnp.clip(e[:, cols], -limit, limit))
                proj[j] = quads(dot(mtcat[...], jnp.concatenate([hi, lo], 1)))

                @pl.when(j > 0)
                def _():
                    pcopy(5 + inner, j, proj.at[j], proj_slots.at[inner, j - 1]).start()
                return carry
            lax.fori_loop(0, n_pts, project, 0)
            if first:
                sweep(gfull, rank // 2, rank)
            finish([pcopy(5 + inner, j, proj.at[j], proj_slots.at[inner, j - 1]) for j in range(1, n_pts)])
            share = proj[0]
            for j in range(1, n_pts):
                share = share + proj_slots[inner, j - 1]
            step = jnp.dot(gfull[...], share, preferred_element_type=F32, precision=lax.Precision.HIGHEST)
            c_out[:, own_cols] = c_out[:, own_cols] - step
            copies = [pcopy(7 + inner, j, c_out.at[:, own_cols], c_out.at[:, own_cols]) for j in range(n_pts - 1, 0, -1)]
            start(copies)
            finish(copies)
            prepare_coefs()

        hi, lo = split(c_out[...].T)
        ctcat[:, :rank] = hi
        ctcat[:, rank:] = lo
        hpart[...] = quads(dot(ccat[...], ctcat[...]))
        hrs = [scopy(3, j, hpart.at[pl.ds(snap_peer(sme, j, n_snap) * hw, hw)], hslots.at[j - 1]) for j in range(1, n_snap)]
        start(hrs)
        hag = [scopy(4, j, hred, hfull.at[pl.ds(sme * hw, hw)]) for j in range(1, n_snap)]

        def hess_share():
            finish(hrs)
            own = hpart[pl.ds(sme * hw, hw), :]
            for j in range(1, n_snap):
                own = own + hslots[j - 1]
            hred[...] = own
            hfull[pl.ds(sme * hw, hw), :] = own
            start(hag)
        limit = find_limit(2, error_pass(), hess_share, nothing)

        def moment(t, carry):
            j = n_snap - 1 - t
            q = snap_peer(sme, j, n_snap)
            part = pl.ds(pl.multiple_of(q * rw, rw), rw)
            hi, lo = split(jnp.clip(e[part, :], -limit, limit))
            mom[j] = quads(dot(jnp.concatenate([hi, lo], 0), ctcat[...]))

            @pl.when(j > 0)
            def _():
                scopy(5, j, mom.at[j], mom_slots.at[j - 1]).start()
            return carry
        lax.fori_loop(0, n_snap, moment, 0)
        finish(hag)
        hfull[...] = hfull[...] + eye
        sweep(hfull, 0, rank)
        finish([scopy(5, j, mom.at[j], mom_slots.at[j - 1]) for j in range(1, n_snap)])
        share = mom[0]
        for j in range(1, n_snap):
            share = share + mom_slots[j - 1]
        step = jnp.dot(share, hfull[...], preferred_element_type=F32, precision=lax.Precision.HIGHEST)
        m_out[own_rows, :] = m_out[own_rows, :] - step
        copies = [scopy(6, j, m_out.at[own_rows], m_out.at[own_rows]) for j in range(1, n_snap)]
        start(copies)
        finish(copies)

        @pl.when(o < OUTER - 1)
        def _():
            prepare_modes()
        return carry
    lax.fori_loop(0, OUTER, outer, 0)
    c_out[...] = c_out[...] * jnp.sqrt(jnp.float32(points))


def shards(n_pts, n_snap, snapshots, modes_init, coefs_init):
    rows, width = snapshots.shape
    rank = modes_init.shape[1]
    cw, rw, gw, hw = width // n_pts, rows // n_snap, rank // n_pts, rank // n_snap
    vmem = pltpu.VMEM
    scratch = [
        vmem((rows, width), F32), vmem((rows, width), F32),
        vmem((rows, 2 * rank), BF16), vmem((2 * rank, rows), BF16),
        vmem((2 * rank, width), BF16), vmem((width, 2 * rank), BF16),
        vmem((8, 256), F32),
        vmem((rank, rank), F32), vmem((n_pts - 1, gw, rank), F32), vmem((gw, rank), F32), vmem((rank, rank), F32),
        vmem((rank, rank), F32), vmem((n_snap - 1, hw, rank), F32), vmem((hw, rank), F32), vmem((rank, rank), F32),
        vmem((3, 8, 128), F32), vmem((3, n_pts - 1, 8, 128), F32),
        vmem((3, 8, 128), F32), vmem((3, n_snap - 1, 8, 128), F32),
        vmem((n_pts, rank, cw), F32), vmem((INNER, n_pts - 1, rank, cw), F32),
        vmem((n_snap, rw, rank), F32), vmem((n_snap - 1, rw, rank), F32),
        pltpu.SemaphoreType.DMA,
        pltpu.SemaphoreType.DMA((9, n_pts - 1)), pltpu.SemaphoreType.DMA((9, n_pts - 1)),
        pltpu.SemaphoreType.DMA((7, n_snap - 1)), pltpu.SemaphoreType.DMA((7, n_snap - 1)),
    ]
    return pl.pallas_call(
        functools.partial(kernel, n_pts, n_snap),
        out_shape=(jax.ShapeDtypeStruct((rows, rank), F32), jax.ShapeDtypeStruct((rank, width), F32)),
        in_specs=[pl.BlockSpec(memory_space=pl.ANY)] + [pl.BlockSpec(memory_space=vmem)] * 2,
        out_specs=(pl.BlockSpec(memory_space=vmem), pl.BlockSpec(memory_space=vmem)),
        scratch_shapes=scratch,
        compiler_params=pltpu.CompilerParams(collective_id=0, has_side_effects=True, vmem_limit_bytes=60 * 1024 * 1024),
    )(snapshots, modes_init, coefs_init)


def solution(mesh):
    in_specs = (P("pts", "snap"), P("pts", None), P(None, "snap"))
    out_specs = (P("pts", None), P(None, "snap"))
    body = functools.partial(shards, mesh.shape["pts"], mesh.shape["snap"])
    return jax.shard_map(body, mesh=mesh, in_specs=in_specs, out_specs=out_specs, check_vma=False)
```

time: 698 us -> 189 us (0.27)
  blocking collectives: 271 us -> 0 us
  waiting for transfers between devices: 191 us -> 0 us
  Pallas kernels: 0 us -> 185 us
  matrix products: 105 us -> 0 us
  other arithmetic: 99.1 us -> 0 us
  between operations: 18.9 us -> 0.64 us
    psum x6 -> x0, blocking collectives: 241 us -> none  [clipped_error(): total = lax.psum(jnp.sum(error * error), ('pts', 'snap'))]
    pallas_call x0 -> x1, Pallas kernels: none -> 185 us  [shards(): pl.pallas_call(functools.partial(kernel, n_pts, n_snap), out_shape=(jax.S...]
    psum x4 -> x0, waiting for transfers between devices: 146 us -> none  [the longest x2 146 us: shards(): summed = lax.psum(moment, 'snap')]
    dot_general x16 -> x0, matrix products: 93.5 us -> none  [high_dot(): jnp.dot(left, right, preferred_element_type=jnp.float32, precision=lax.Pr...]
    another operation x20 -> x0, other arithmetic: 91.4 us -> none  [the longest x6 24.8 us: shards(): factor = jnp.linalg.cholesky(gram)]
    reduce_scatter x4 -> x0, waiting for transfers between devices: 44.4 us -> none  [shards(): share = lax.psum_scatter(product, 'pts', scatter_dimension=1, tiled=True)]
    all_gather x4 -> x0, blocking collectives: 29.3 us -> none  [shards(): coefs = lax.all_gather(own, 'pts', axis=1, tiled=True)]
    another operation x12 -> x0, matrix products: 11.3 us -> none  [the longest x8 6.8 us: shards(): own = own + jax.scipy.linalg.cho_solve((factor, True), share)]
  transfers between devices with their start and end apart: 8 -> 0, of which waited for: 4 -> 0; matrix products, arithmetic and copies ran while one was open for 12% -> 0% of each run, Pallas kernels for 0% -> 0%
where the time goes in v1:
time: 189 us
  Pallas kernels  185 us (98%)
  local copies, waits for them, and re-layouts  3.75 us (2%)
    pallas_call x1, Pallas kernels, shards(): pl.pallas_call(functools.partial(kernel, n_pts, n_snap), out_shape=(jax.S...  185 us

profile of v1, /device:TPU:0, one launch (start us, length us, event | category | flops | bytes accessed | tf_op | source)
XLA Modules:
  0.0 189.1 jit_solution(7872947618517468897)
XLA Ops:
  0.6 184.7 %shard_map.50 = (f32[1024,128]{1,0:T(8,128)}, f32[128,1024]{1,0:T(8,128)}) custom-call(f32[1024,1024]{1,0:T(8,128)} %s_hbm.1, f32[1024,128]{1,0:T(8,128)} %m_in.1, f32[128,1024]{1,0:T(8,128)} %c_in.1), custom_call_target="tpu_custom_call" | custom-call | tf_op jit(solution)/shard_map/pallas_call | solution.py:299
  185.3 1.9 copy.7
  187.2 1.9 copy.8

commit v2 on v1

--- a/solution.py
+++ b/solution.py
@@ -9,6 +9,8 @@
 
 OUTER = 2
 INNER = 2
+PIVOTS = 4
+CHUNK = 128
 
 HUBER = 1.345
 RIDGE = 0.01
@@ -47,21 +49,23 @@
 def kernel(n_pts, n_snap, s_hbm, m_in, c_in, m_out, c_out,
            s, e, mcat, mtcat, ccat, ctcat, sq,
            gpart, gslots, gred, gfull, hpart, hslots, hred, hfull,
-           tile_p, slots_p, tile_s, slots_s, proj, proj_slots, mom, mom_slots,
-           load_sem, p_send, p_recv, s_send, s_recv):
+           tile_p, slots_p, tile_s, slots_s, cpart, cslots, xslots, ypart, yslots, zpart, zslots,
+           load_sem, p_send, p_recv, s_send, s_recv, c_send, c_recv, x_send, x_recv,
+           y_send, y_recv, z_send, z_recv):
     rows, width = s.shape
     rank = m_in.shape[1]
     pme = lax.axis_index("pts")
     sme = lax.axis_index("snap")
-    cw = width // n_pts
     rw = rows // n_snap
+    half = width // 2
+    chunks = half // CHUNK
+    n_x, n_z = n_pts // 2, n_snap // 2
+    px, core = pme // 2, lax.rem(pme, 2)
+    sz, sy = sme // 2, lax.rem(sme, 2)
     gw = rank // n_pts
     hw = rank // n_snap
-    points = float(rows * n_pts)
     count = float(rows * n_pts * width * n_snap)
     step_cols = 256
-    own_cols = pl.ds(pl.multiple_of(pme * cw, cw), cw)
-    own_rows = pl.ds(pl.multiple_of(sme * rw, rw), rw)
 
     load = pltpu.make_async_copy(s_hbm, s, load_sem)
     load.start()
@@ -85,6 +89,33 @@
             src_ref=src, dst_ref=dst, send_sem=s_send.at[site, j - 1], recv_sem=s_recv.at[site, j - 1],
             device_id={"snap": snap_peer(sme, j, n_snap)}, device_id_type=MESH)
 
+    def ccopy(site, k, src, dst):
+        return pltpu.make_async_remote_copy(
+            src_ref=src, dst_ref=dst, send_sem=c_send.at[site, k], recv_sem=c_recv.at[site, k],
+            device_id={"pts": px * 2 + 1 - core}, device_id_type=MESH)
+
+    def xcopy(site, k, d):
+        ref = xslots.at[site, px, k]
+        return pltpu.make_async_remote_copy(
+            src_ref=ref, dst_ref=ref, send_sem=x_send.at[site, k, d - 1], recv_sem=x_recv.at[site, k, d - 1],
+            device_id={"pts": lax.rem(px + d, n_x) * 2 + core}, device_id_type=MESH)
+
+    def ycopy(site, d, src, dst):
+        return pltpu.make_async_remote_copy(
+            src_ref=src, dst_ref=dst, send_sem=y_send.at[site, d], recv_sem=y_recv.at[site, d],
+            device_id={"snap": sz * 2 + 1 - sy}, device_id_type=MESH)
+
+    def zcopy(site, d, src, dst):
+        return pltpu.make_async_remote_copy(
+            src_ref=src, dst_ref=dst, send_sem=z_send.at[site, d - 1], recv_sem=z_recv.at[site, d - 1],
+            device_id={"snap": lax.rem(sz + d, n_z) * 2 + sy}, device_id_type=MESH)
+
+    def col_chunk(which, k):
+        return pl.ds(pl.multiple_of(which * half + k * CHUNK, CHUNK), CHUNK)
+
+    def row_block(d, which):
+        return pl.ds(pl.multiple_of((lax.rem(sz + d, n_z) * 2 + which) * rw, rw), rw)
+
     def start(copies):
         for copy in copies:
             copy.start()
@@ -113,19 +144,32 @@
         lane = lax.broadcasted_iota(jnp.int32, (rank, rank), 1)
         sub = lax.broadcasted_iota(jnp.int32, (rank, rank), 0)
         lane_row = lax.broadcasted_iota(jnp.int32, (1, rank), 1)
-
-        def body(k, carry):
+        sub_col = lax.broadcasted_iota(jnp.int32, (rank, 1), 0)
+
+        def body(t, carry):
+            k = t * PIVOTS
             full = ref[...]
-            row = ref[pl.ds(k, 1), :]
-            pivot = jnp.sum(jnp.where(lane_row == k, row, 0.0), axis=1, keepdims=True)
-            col = jnp.sum(jnp.where(lane == k, full, 0.0), axis=1, keepdims=True)
-            inv = 1.0 / pivot
-            rowd = jnp.where(lane_row == k, -inv, row * inv)
-            new = full - col * (row * inv)
-            new = jnp.where(lane == k, col * inv, new)
-            ref[...] = jnp.where(sub == k, rowd, new)
+            cols = [jnp.sum(jnp.where(lane == k + p, full, 0.0), axis=1, keepdims=True) for p in range(PIVOTS)]
+            rws = [ref[pl.ds(k + p, 1), :] for p in range(PIVOTS)]
+            blk = {}
+            for p in range(PIVOTS):
+                for q in range(p, PIVOTS):
+                    blk[p, q] = jnp.sum(jnp.where(lane_row == k + q, rws[p], 0.0), axis=1, keepdims=True)
+            for p in range(PIVOTS):
+                inv = 1.0 / blk[p, p]
+                row, col = rws[p], cols[p]
+                for q in range(p + 1, PIVOTS):
+                    f = blk[p, q] * inv
+                    rws[q] = jnp.where(lane_row == k + p, f, rws[q] - f * row)
+                    cols[q] = jnp.where(sub_col == k + p, f, cols[q] - f * col)
+                    for u in range(q, PIVOTS):
+                        blk[q, u] = blk[q, u] - f * blk[p, u]
+                rowd = row * inv
+                full = jnp.where(lane == k + p, col * inv, full - col * rowd)
+                full = jnp.where(sub == k + p, jnp.where(lane_row == k + p, -inv, rowd), full)
+            ref[...] = full
             return carry
-        lax.fori_loop(lo, hi, body, 0)
+        lax.fori_loop(lo // PIVOTS, hi // PIVOTS, body, 0)
 
     def error_pass():
         sq[...] = jnp.zeros_like(sq)
@@ -200,29 +244,55 @@
             first = inner == 0
             limit = find_limit(inner, acc, gram_share if first else nothing, gram_sweep if first else nothing)
 
-            def project(t, carry):
-                j = n_pts - 1 - t
-                q = pts_peer(pme, j, n_pts)
-                cols = pl.ds(pl.multiple_of(q * cw, cw), cw)
+            def product(cols):
                 hi, lo = split(jnp.clip(e[:, cols], -limit, limit))
-                proj[j] = quads(dot(mtcat[...], jnp.concatenate([hi, lo], 1)))
-
-                @pl.when(j > 0)
-                def _():
-                    pcopy(5 + inner, j, proj.at[j], proj_slots.at[inner, j - 1]).start()
+                return quads(dot(mtcat[...], jnp.concatenate([hi, lo], 1)))
+
+            def give(k):
+                return ccopy(inner, k, cpart.at[k], cslots.at[inner, k])
+
+            def spread(k):
+                ref = c_out.at[:, col_chunk(core, k)]
+                return ccopy(INNER + inner, k, ref, ref)
+
+            def theirs(k, carry):
+                cpart[k] = product(col_chunk(1 - core, k))
+                give(k).start()
                 return carry
-            lax.fori_loop(0, n_pts, project, 0)
+            lax.fori_loop(0, chunks, theirs, 0)
+
+            def ours(k, carry):
+                mine = product(col_chunk(core, k))
+                give(k).wait_recv()
+                xslots[inner, px, k] = mine + cslots[inner, k]
+                for d in range(1, n_x):
+                    xcopy(inner, k, d).start()
+                return carry
+            lax.fori_loop(0, chunks, ours, 0)
             if first:
                 sweep(gfull, rank // 2, rank)
-            finish([pcopy(5 + inner, j, proj.at[j], proj_slots.at[inner, j - 1]) for j in range(1, n_pts)])
-            share = proj[0]
-            for j in range(1, n_pts):
-                share = share + proj_slots[inner, j - 1]
-            step = jnp.dot(gfull[...], share, preferred_element_type=F32, precision=lax.Precision.HIGHEST)
-            c_out[:, own_cols] = c_out[:, own_cols] - step
-            copies = [pcopy(7 + inner, j, c_out.at[:, own_cols], c_out.at[:, own_cols]) for j in range(n_pts - 1, 0, -1)]
-            start(copies)
-            finish(copies)
+
+            def update(k, carry):
+                for d in range(1, n_x):
+                    xcopy(inner, k, d).wait_recv()
+                share = xslots[inner, 0, k]
+                for x in range(1, n_x):
+                    share = share + xslots[inner, x, k]
+                step = jnp.dot(gfull[...], share, preferred_element_type=F32, precision=lax.Precision.HIGHEST)
+                cols = col_chunk(core, k)
+                c_out[:, cols] = c_out[:, cols] - step
+                spread(k).start()
+                return carry
+            lax.fori_loop(0, chunks, update, 0)
+
+            def settle(k, carry):
+                spread(k).wait_recv()
+                spread(k).wait_send()
+                give(k).wait_send()
+                for d in range(1, n_x):
+                    xcopy(inner, k, d).wait_send()
+                return carry
+            lax.fori_loop(0, chunks, settle, 0)
             prepare_coefs()
 
         hi, lo = split(c_out[...].T)
@@ -243,43 +313,81 @@
             start(hag)
         limit = find_limit(2, error_pass(), hess_share, nothing)
 
-        def moment(t, carry):
-            j = n_snap - 1 - t
-            q = snap_peer(sme, j, n_snap)
-            part = pl.ds(pl.multiple_of(q * rw, rw), rw)
+        def moment(part):
             hi, lo = split(jnp.clip(e[part, :], -limit, limit))
-            mom[j] = quads(dot(jnp.concatenate([hi, lo], 0), ctcat[...]))
-
-            @pl.when(j > 0)
+            return quads(dot(jnp.concatenate([hi, lo], 0), ctcat[...]))
+
+        def over_y(d):
+            return ycopy(0, d, ypart.at[d], yslots.at[d])
+
+        def over_z(d):
+            return zcopy(0, d, zpart.at[d], zslots.at[d - 1])
+
+        def theirs(t, carry):
+            d = n_z - 1 - t
+            ypart[d] = moment(row_block(d, 1 - sy))
+            over_y(d).start()
+            return carry
+        lax.fori_loop(0, n_z, theirs, 0)
+
+        def ours(t, carry):
+            d = n_z - 1 - t
+            mine = moment(row_block(d, sy))
+            over_y(d).wait_recv()
+            zpart[d] = mine + yslots[d]
+
+            @pl.when(d > 0)
             def _():
-                scopy(5, j, mom.at[j], mom_slots.at[j - 1]).start()
+                over_z(d).start()
             return carry
-        lax.fori_loop(0, n_snap, moment, 0)
+        lax.fori_loop(0, n_z, ours, 0)
         finish(hag)
         hfull[...] = hfull[...] + eye
         sweep(hfull, 0, rank)
-        finish([scopy(5, j, mom.at[j], mom_slots.at[j - 1]) for j in range(1, n_snap)])
-        share = mom[0]
-        for j in range(1, n_snap):
-            share = share + mom_slots[j - 1]
+        for d in range(1, n_z):
+            over_z(d).wait_recv()
+        share = zpart[0]
+        for d in range(1, n_z):
+            share = share + zslots[d - 1]
         step = jnp.dot(share, hfull[...], preferred_element_type=F32, precision=lax.Precision.HIGHEST)
+        own_rows = row_block(0, sy)
         m_out[own_rows, :] = m_out[own_rows, :] - step
-        copies = [scopy(6, j, m_out.at[own_rows], m_out.at[own_rows]) for j in range(1, n_snap)]
-        start(copies)
-        finish(copies)
+        own_ref = m_out.at[own_rows]
+        order = sorted(range(1, n_z), key=lambda d: -min(d, n_z - d))
+        for d in order:
+            zcopy(1, d, own_ref, own_ref).start()
+        ycopy(1, 0, own_ref, own_ref).start()
+
+        def pass_on(d):
+            ref = m_out.at[row_block(n_z - d, sy)]
+            return ycopy(1, d, ref, ref)
+        for d in sorted(range(1, n_z), key=lambda d: min(d, n_z - d)):
+            zcopy(1, d, own_ref, own_ref).wait_recv()
+            pass_on(d).start()
+        ycopy(1, 0, own_ref, own_ref).wait_recv()
+        for d in range(1, n_z):
+            pass_on(d).wait_recv()
+        ycopy(1, 0, own_ref, own_ref).wait_send()
+        over_y(0).wait_send()
+        for d in range(1, n_z):
+            pass_on(d).wait_send()
+            over_y(d).wait_send()
+            over_z(d).wait_send()
+            zcopy(1, d, own_ref, own_ref).wait_send()
 
         @pl.when(o < OUTER - 1)
         def _():
             prepare_modes()
         return carry
     lax.fori_loop(0, OUTER, outer, 0)
-    c_out[...] = c_out[...] * jnp.sqrt(jnp.float32(points))
 
 
 def shards(n_pts, n_snap, snapshots, modes_init, coefs_init):
     rows, width = snapshots.shape
     rank = modes_init.shape[1]
-    cw, rw, gw, hw = width // n_pts, rows // n_snap, rank // n_pts, rank // n_snap
+    rw, gw, hw = rows // n_snap, rank // n_pts, rank // n_snap
+    chunks, n_x, n_z = width // 2 // CHUNK, n_pts // 2, n_snap // 2
+    points = float(rows * n_pts)
     vmem = pltpu.VMEM
     scratch = [
         vmem((rows, width), F32), vmem((rows, width), F32),
@@ -290,13 +398,19 @@
         vmem((rank, rank), F32), vmem((n_snap - 1, hw, rank), F32), vmem((hw, rank), F32), vmem((rank, rank), F32),
         vmem((3, 8, 128), F32), vmem((3, n_pts - 1, 8, 128), F32),
         vmem((3, 8, 128), F32), vmem((3, n_snap - 1, 8, 128), F32),
-        vmem((n_pts, rank, cw), F32), vmem((INNER, n_pts - 1, rank, cw), F32),
-        vmem((n_snap, rw, rank), F32), vmem((n_snap - 1, rw, rank), F32),
+        vmem((chunks, rank, CHUNK), F32), vmem((INNER, chunks, rank, CHUNK), F32),
+        vmem((INNER, n_x, chunks, rank, CHUNK), F32),
+        vmem((n_z, rw, rank), F32), vmem((n_z, rw, rank), F32),
+        vmem((n_z, rw, rank), F32), vmem((n_z - 1, rw, rank), F32),
         pltpu.SemaphoreType.DMA,
-        pltpu.SemaphoreType.DMA((9, n_pts - 1)), pltpu.SemaphoreType.DMA((9, n_pts - 1)),
-        pltpu.SemaphoreType.DMA((7, n_snap - 1)), pltpu.SemaphoreType.DMA((7, n_snap - 1)),
+        pltpu.SemaphoreType.DMA((5, n_pts - 1)), pltpu.SemaphoreType.DMA((5, n_pts - 1)),
+        pltpu.SemaphoreType.DMA((5, n_snap - 1)), pltpu.SemaphoreType.DMA((5, n_snap - 1)),
+        pltpu.SemaphoreType.DMA((2 * INNER, chunks)), pltpu.SemaphoreType.DMA((2 * INNER, chunks)),
+        pltpu.SemaphoreType.DMA((INNER, chunks, n_x - 1)), pltpu.SemaphoreType.DMA((INNER, chunks, n_x - 1)),
+        pltpu.SemaphoreType.DMA((2, n_z)), pltpu.SemaphoreType.DMA((2, n_z)),
+        pltpu.SemaphoreType.DMA((2, n_z - 1)), pltpu.SemaphoreType.DMA((2, n_z - 1)),
     ]
-    return pl.pallas_call(
+    modes, coefs = pl.pallas_call(
         functools.partial(kernel, n_pts, n_snap),
         out_shape=(jax.ShapeDtypeStruct((rows, rank), F32), jax.ShapeDtypeStruct((rank, width), F32)),
         in_specs=[pl.BlockSpec(memory_space=pl.ANY)] + [pl.BlockSpec(memory_space=vmem)] * 2,
@@ -304,6 +418,7 @@
         scratch_shapes=scratch,
         compiler_params=pltpu.CompilerParams(collective_id=0, has_side_effects=True, vmem_limit_bytes=60 * 1024 * 1024),
     )(snapshots, modes_init, coefs_init)
+    return modes, coefs * jnp.sqrt(jnp.float32(points))
 
 
 def solution(mesh):

time: 189 us -> 158 us (0.84)
  Pallas kernels: 185 us -> 153 us
    pallas_call x1, Pallas kernels: 185 us -> 153 us  [shards(): pl.pallas_call(functools.partial(kernel, n_pts, n_snap), out_shape=(jax.S...]
where the time goes in v2:
time: 158 us
  Pallas kernels  153 us (97%)
  other arithmetic  1.88 us (1%)
  local copies, waits for them, and re-layouts  1.87 us (1%)
    pallas_call x1, Pallas kernels, shards(): pl.pallas_call(functools.partial(kernel, n_pts, n_snap), out_shape=(jax.S...  153 us

profile of v2, /device:TPU:0, one launch (start us, length us, event | category | flops | bytes accessed | tf_op | source)
XLA Modules:
  0.0 157.5 jit_solution(13151834110801783386)
XLA Ops:
  0.6 153.1 %shard_map.50 = (f32[1024,128]{1,0:T(8,128)}, f32[128,1024]{1,0:T(8,128)}) custom-call(f32[1024,1024]{1,0:T(8,128)} %s_hbm.1, f32[1024,128]{1,0:T(8,128)} %m_in.1, f32[128,1024]{1,0:T(8,128)} %c_in.1), custom_call_target="tpu_custom_call" | custom-call | tf_op jit(solution)/shard_map/pallas_call | solution.py:413
  153.8 1.9 %broadcast_multiply_fusion = f32[128,1024]{1,0:T(8,128)} fusion(f32[128,1024]{1,0:T(8,128)} %get-tuple-element.5), kind=kLoop, calls=%fused_computation | loop fusion | flops 131072 | bytes 1048576 | tf_op jit(solution)/shard_map/mul | solution.py:421
  155.6 1.9 %copy.6 = f32[1024,128]{1,0:T(8,128)} copy(f32[1024,128]{1,0:T(8,128)} %get-tuple-element.8) | data formatting | bytes 1048576

commit v3 on v2

--- a/solution.py
+++ b/solution.py
@@ -140,14 +140,14 @@
         ccat[:rank, :] = hi
         ccat[rank:, :] = lo
 
-    def sweep(ref, lo, hi):
+    def sweep(ref, base, steps):
         lane = lax.broadcasted_iota(jnp.int32, (rank, rank), 1)
         sub = lax.broadcasted_iota(jnp.int32, (rank, rank), 0)
         lane_row = lax.broadcasted_iota(jnp.int32, (1, rank), 1)
         sub_col = lax.broadcasted_iota(jnp.int32, (rank, 1), 0)
 
         def body(t, carry):
-            k = t * PIVOTS
+            k = (base + t) * PIVOTS
             full = ref[...]
             cols = [jnp.sum(jnp.where(lane == k + p, full, 0.0), axis=1, keepdims=True) for p in range(PIVOTS)]
             rws = [ref[pl.ds(k + p, 1), :] for p in range(PIVOTS)]
@@ -169,7 +169,7 @@
                 full = jnp.where(sub == k + p, jnp.where(lane_row == k + p, -inv, rowd), full)
             ref[...] = full
             return carry
-        lax.fori_loop(lo // PIVOTS, hi // PIVOTS, body, 0)
+        lax.fori_loop(0, steps, body, 0)
 
     def error_pass():
         sq[...] = jnp.zeros_like(sq)
@@ -240,7 +240,7 @@
             def gram_sweep():
                 finish(gag)
                 gfull[...] = gfull[...] + eye
-                sweep(gfull, 0, rank // 2)
+                sweep(gfull, 0, rank // PIVOTS // 2)
             first = inner == 0
             limit = find_limit(inner, acc, gram_share if first else nothing, gram_sweep if first else nothing)
 
@@ -270,7 +270,7 @@
                 return carry
             lax.fori_loop(0, chunks, ours, 0)
             if first:
-                sweep(gfull, rank // 2, rank)
+                sweep(gfull, rank // PIVOTS // 2, rank // PIVOTS // 2)
 
             def update(k, carry):
                 for d in range(1, n_x):
@@ -330,9 +330,14 @@
             return carry
         lax.fori_loop(0, n_z, theirs, 0)
 
+        finish(hag)
+        hfull[...] = hfull[...] + eye
+        early = rank // PIVOTS // 2 // n_z
+
         def ours(t, carry):
             d = n_z - 1 - t
             mine = moment(row_block(d, sy))
+            sweep(hfull, t * early, early)
             over_y(d).wait_recv()
             zpart[d] = mine + yslots[d]
 
@@ -341,9 +346,7 @@
                 over_z(d).start()
             return carry
         lax.fori_loop(0, n_z, ours, 0)
-        finish(hag)
-        hfull[...] = hfull[...] + eye
-        sweep(hfull, 0, rank)
+        sweep(hfull, early * n_z, rank // PIVOTS - early * n_z)
         for d in range(1, n_z):
             over_z(d).wait_recv()
         share = zpart[0]

time: 158 us -> 153 us (0.968)
  Pallas kernels: 153 us -> 148 us
    pallas_call x1, Pallas kernels: 153 us -> 148 us  [shards(): pl.pallas_call(functools.partial(kernel, n_pts, n_snap), out_shape=(jax.S...]
where the time goes in v3:
time: 153 us
  Pallas kernels  148 us (97%)
  other arithmetic  1.88 us (1%)
  local copies, waits for them, and re-layouts  1.87 us (1%)
    pallas_call x1, Pallas kernels, shards(): pl.pallas_call(functools.partial(kernel, n_pts, n_snap), out_shape=(jax.S...  148 us

profile of v3, /device:TPU:0, one launch (start us, length us, event | category | flops | bytes accessed | tf_op | source)
XLA Modules:
  0.0 152.5 jit_solution(10220369204819855213)
XLA Ops:
  0.6 148.2 %shard_map.50 = (f32[1024,128]{1,0:T(8,128)}, f32[128,1024]{1,0:T(8,128)}) custom-call(f32[1024,1024]{1,0:T(8,128)} %s_hbm.1, f32[1024,128]{1,0:T(8,128)} %m_in.1, f32[128,1024]{1,0:T(8,128)} %c_in.1), custom_call_target="tpu_custom_call" | custom-call | tf_op jit(solution)/shard_map/pallas_call | solution.py:416
  148.8 1.9 %broadcast_multiply_fusion = f32[128,1024]{1,0:T(8,128)} fusion(f32[128,1024]{1,0:T(8,128)} %get-tuple-element.5), kind=kLoop, calls=%fused_computation | loop fusion | flops 131072 | bytes 1048576 | tf_op jit(solution)/shard_map/mul | solution.py:424
  150.7 1.9 %copy.6 = f32[1024,128]{1,0:T(8,128)} copy(f32[1024,128]{1,0:T(8,128)} %get-tuple-element.8) | data formatting | bytes 1048576
